TPU v7x, 32 devices: a whole 2x2x4 slice. The times are simulated.
32 devices in a mesh: dp: 16 (over z, x, core), mp: 2 (over y).
Axes of the slice: x: 2, y: 2, z: 4, core: 2. Of those that a mesh axis runs over, the one named last changes fastest.
Arguments:
- inputs: bfloat16 [32768, 768], P(('dp', 'mp')), may hold values from -12 to 12
- segments: int32 [32768], P('dp'), may hold values from -1 to 9, as said below
- w_qkv: bfloat16 [3, 768, 768], P(None, 'dp', 'mp'), may hold values from -0.21875 to 0.21875
- w_out: bfloat16 [768, 768], P('mp', 'dp'), may hold values from -4 to 4
- first_gain: bfloat16 [768], P('dp'), may hold values from 0.5 to 1.5
- first_bias: bfloat16 [768], P('dp'), may hold values from -3 to 3
- w_gate: bfloat16 [768, 3072], P('dp', 'mp'), may hold values from -0.21875 to 0.21875
- w_up: bfloat16 [768, 3072], P('dp', 'mp'), may hold values from -0.21875 to 0.21875
- w_down: bfloat16 [3072, 768], P('mp', 'dp'), may hold values from -0.109375 to 0.109375
- second_gain: bfloat16 [768], P('dp'), may hold values from 0.5 to 1.5
- second_bias: bfloat16 [768], P('dp'), may hold values from -3 to 3
- d_out: bfloat16 [32768, 768], P(('dp', 'mp')), may hold values from -12 to 12
Outputs:
- outputs: bfloat16 [32768, 768], P(('dp', 'mp'))
- grad_inputs: float32 [32768, 768], P(('dp', 'mp'))
- grad_w_qkv: float32 [3, 768, 768], P(None, 'dp', 'mp')
- grad_w_out: float32 [768, 768], P('mp', 'dp')
- grad_first_gain: float32 [768], P('dp')
- grad_first_bias: float32 [768], P('dp')
- grad_w_gate: float32 [768, 3072], P('dp', 'mp')
- grad_w_up: float32 [768, 3072], P('dp', 'mp')
- grad_w_down: float32 [3072, 768], P('mp', 'dp')
- grad_second_gain: float32 [768], P('dp')
- grad_second_bias: float32 [768], P('dp')
Inputs may be any that keep to these rules, and one draw needn't show every extreme that they name: `segments`: within each sequence of 2048 tokens, tokens carry the number of their document, counting from 0 in order; each document has 200 to 2000 tokens; the tokens after the last whole document are padding, marked -1, and every sequence ends with one or more of them. In the first sequence every document has exactly 200 tokens.
All inputs are finite; a program needn't handle non-finite values.
Results may differ from a plain program's by a relative error of at most 0.017.
The roundings to bfloat16 on the way count: a program that leaves them out, or rounds other values in their place, can miss the bound.
Values may be sent and summed in bfloat16 or wider, within the bound.
A program may use at most 192 MiB of HBM per device.

v0:
```python
import jax
import jax.numpy as jnp
from jax import lax
from jax.sharding import PartitionSpec as P

HEAD_DIM = 64
SEQ_LEN = 2048


EPSILON = 1e-12
ROPE_BASE = 1000.0
MASKED = -10000.0


def rope_tables(seq_len, head_dim):
    half_dim = head_dim // 2
    frequency = ROPE_BASE ** (-2.0 * jnp.arange(half_dim, dtype=jnp.float32) / head_dim)
    angles = jnp.arange(seq_len, dtype=jnp.float32)[:, None] * frequency[None, :]
    return (jnp.cos(angles), jnp.sin(angles))


def rotate(values, cos_table, sin_table):
    half_dim = values.shape[-1] // 2
    front_half = values[..., :half_dim]
    back_half = values[..., half_dim:]
    return jnp.concatenate(
        [
            front_half * cos_table - back_half * sin_table,
            back_half * cos_table + front_half * sin_table,
        ],
        axis=-1,
    )


def contract_rows(left_op, right_op):
    return lax.dot_general(
        left_op, right_op, (((0,), (0,)), ((), ())), preferred_element_type=jnp.float32
    )


def contract_cols(left_op, right_op):
    return lax.dot_general(
        left_op, right_op, (((1,), (1,)), ((), ())), preferred_element_type=jnp.float32
    )


def norm_forward(hidden, norm_gain, norm_bias):
    centered = hidden - jnp.mean(hidden, axis=-1, keepdims=True)
    inv_std = lax.rsqrt(jnp.mean(centered * centered, axis=-1, keepdims=True) + EPSILON)
    normed = centered * inv_std
    return (normed * norm_gain + norm_bias, normed, inv_std)


def norm_back(grad_y, normed, inv_std, norm_gain):
    grad_gain = jnp.sum(grad_y * normed, axis=0)
    grad_bias = jnp.sum(grad_y, axis=0)
    scaled = grad_y * norm_gain
    grad_h = inv_std * (
        scaled
        - jnp.mean(scaled, axis=-1, keepdims=True)
        - normed * jnp.mean(scaled * normed, axis=-1, keepdims=True)
    )
    return (grad_h, grad_gain, grad_bias)


def block_scores(q_block, key_rot, seg_block, seg_all, score_scale):
    scores = contract_cols(q_block, key_rot) * score_scale
    allowed = (seg_block[:, None] == seg_all[None, :]) & (seg_block[:, None] >= 0)
    return (jnp.where(allowed, scores, MASKED), allowed.astype(jnp.float32))


def attend_forward(queries, key_rot, values, seg_rows, head_count, score_scale):
    seq_len = queries.shape[1]
    block_len = min(512, seq_len)
    blocks = seq_len // block_len

    def one_pair(pair_index):
        query_one = queries[pair_index]
        key_one = key_rot[pair_index]
        value_one = values[pair_index]
        seg_one = seg_rows[pair_index // head_count]

        def one_block(block_index):
            offset = block_index * block_len
            q_block = lax.dynamic_slice_in_dim(query_one, offset, block_len, 0)
            seg_block = lax.dynamic_slice_in_dim(seg_one, offset, block_len, 0)
            masked, allowed = block_scores(q_block, key_one, seg_block, seg_one, score_scale)
            row_max = jnp.max(masked, axis=1)
            exponent = jnp.exp(masked - row_max[:, None]) * allowed
            row_sum = jnp.sum(exponent, axis=1)
            weights = (exponent / jnp.maximum(row_sum, 1.0)[:, None]).astype(jnp.bfloat16)
            return (
                jnp.dot(weights, value_one, preferred_element_type=jnp.float32),
                row_max,
                row_sum,
            )

        block_out, row_max, row_sum = lax.map(one_block, jnp.arange(blocks))
        return (block_out.reshape(seq_len, -1), row_max.reshape(seq_len), row_sum.reshape(seq_len))

    return lax.map(one_pair, jnp.arange(queries.shape[0]))


def attend_backward(
    queries, key_rot, values, seg_rows, head_count, score_scale, row_max, row_sum, grad_att
):
    seq_len = queries.shape[1]
    head_dim = queries.shape[2]
    block_len = min(512, seq_len)
    blocks = seq_len // block_len

    def one_pair(pair_index):
        query_one = queries[pair_index]
        key_one = key_rot[pair_index]
        value_one = values[pair_index]
        seg_one = seg_rows[pair_index // head_count]
        max_one = row_max[pair_index]
        sum_one = row_sum[pair_index]
        grad_one = grad_att[pair_index]

        def one_block(running, block_index):
            key_grad, value_grad = running
            offset = block_index * block_len
            q_block = lax.dynamic_slice_in_dim(query_one, offset, block_len, 0)
            seg_block = lax.dynamic_slice_in_dim(seg_one, offset, block_len, 0)
            max_block = lax.dynamic_slice_in_dim(max_one, offset, block_len, 0)
            sum_block = lax.dynamic_slice_in_dim(sum_one, offset, block_len, 0)
            grad_block = lax.dynamic_slice_in_dim(grad_one, offset, block_len, 0)
            masked, allowed = block_scores(q_block, key_one, seg_block, seg_one, score_scale)
            exponent = jnp.exp(masked - max_block[:, None]) * allowed
            weights = exponent / jnp.maximum(sum_block, 1.0)[:, None]
            value_grad = value_grad + contract_rows(weights.astype(jnp.bfloat16), grad_block)
            prob_grad = contract_cols(grad_block, value_one)
            inner = jnp.sum(weights * prob_grad, axis=1, keepdims=True)
            score_grad = (weights * (prob_grad - inner)).astype(jnp.bfloat16)
            query_grad = (
                jnp.dot(score_grad, key_one, preferred_element_type=jnp.float32) * score_scale
            )
            key_grad = key_grad + contract_rows(score_grad, q_block) * score_scale
            return ((key_grad, value_grad), query_grad)

        zeros_init = jnp.zeros((seq_len, head_dim), jnp.float32)
        (key_grad, value_grad), query_grads = lax.scan(
            one_block, (zeros_init, zeros_init), jnp.arange(blocks)
        )
        return (query_grads.reshape(seq_len, head_dim), key_grad, value_grad)

    return lax.map(one_pair, jnp.arange(queries.shape[0]))


def on_device(
    inputs,
    segments,
    w_qkv,
    w_out,
    first_gain,
    first_bias,
    w_gate,
    w_up,
    w_down,
    second_gain,
    second_bias,
    d_out,
):
    qkv_full, out_full, gain_one, bias_one = (
        lax.all_gather(w_qkv, "dp", axis=1, tiled=True),
        lax.all_gather(w_out, "dp", axis=1, tiled=True),
        lax.all_gather(first_gain, "dp", axis=0, tiled=True),
        lax.all_gather(first_bias, "dp", axis=0, tiled=True),
    )
    gate_full, up_full, down_full, gain_two, bias_two = (
        lax.all_gather(w_gate, "dp", axis=0, tiled=True),
        lax.all_gather(w_up, "dp", axis=0, tiled=True),
        lax.all_gather(w_down, "dp", axis=1, tiled=True),
        lax.all_gather(second_gain, "dp", axis=0, tiled=True),
        lax.all_gather(second_bias, "dp", axis=0, tiled=True),
    )
    gain_one = gain_one.astype(jnp.float32)
    bias_one = bias_one.astype(jnp.float32)
    gain_two = gain_two.astype(jnp.float32)
    bias_two = bias_two.astype(jnp.float32)
    local_heads = w_qkv.shape[2] // HEAD_DIM
    score_scale = HEAD_DIM ** (-0.5)
    rows_all = lax.all_gather(inputs, "mp", axis=0, tiled=True)
    seq_count = rows_all.shape[0] // SEQ_LEN
    seg_rows = segments.reshape(seq_count, SEQ_LEN)
    cos_table, sin_table = rope_tables(SEQ_LEN, HEAD_DIM)

    def to_heads(tensor):
        return (
            tensor.reshape(seq_count, SEQ_LEN, local_heads, HEAD_DIM)
            .transpose(0, 2, 1, 3)
            .reshape(seq_count * local_heads, SEQ_LEN, HEAD_DIM)
        )

    def from_heads(tensor):
        return (
            tensor.reshape(seq_count, local_heads, SEQ_LEN, HEAD_DIM)
            .transpose(0, 2, 1, 3)
            .reshape(seq_count * SEQ_LEN, local_heads * HEAD_DIM)
        )

    projected = jnp.einsum("sd,kdc->ksc", rows_all, qkv_full, preferred_element_type=jnp.float32)
    queries = rotate(to_heads(projected[0]), cos_table, sin_table).astype(jnp.bfloat16)
    key_rot = rotate(to_heads(projected[1]), cos_table, sin_table).astype(jnp.bfloat16)
    values = to_heads(projected[2].astype(jnp.bfloat16))
    attended, row_max, row_sum = attend_forward(
        queries, key_rot, values, seg_rows, local_heads, score_scale
    )
    merged = from_heads(attended.astype(jnp.bfloat16))
    attn_part = lax.psum_scatter(
        jnp.dot(merged, out_full, preferred_element_type=jnp.float32),
        "mp",
        scatter_dimension=0,
        tiled=True,
    )
    middle, first_hat, first_inv = norm_forward(
        inputs.astype(jnp.float32) + attn_part, gain_one, bias_one
    )
    middle_all = lax.all_gather(middle.astype(jnp.bfloat16), "mp", axis=0, tiled=True)
    gate_act = jnp.dot(middle_all, gate_full, preferred_element_type=jnp.float32)
    up_act = jnp.dot(middle_all, up_full, preferred_element_type=jnp.float32)
    sigmoid_gate = jax.nn.sigmoid(gate_act)
    silu_gate = gate_act * sigmoid_gate
    hidden = (silu_gate * up_act).astype(jnp.bfloat16)
    mlp_part = lax.psum_scatter(
        jnp.dot(hidden, down_full, preferred_element_type=jnp.float32),
        "mp",
        scatter_dimension=0,
        tiled=True,
    )
    result, second_hat, second_inv = norm_forward(middle + mlp_part, gain_two, bias_two)
    outputs = result.astype(jnp.bfloat16)
    grad_two, second_gain_part, second_bias_part = norm_back(
        d_out.astype(jnp.float32), second_hat, second_inv, gain_two
    )
    grad_two_all = lax.all_gather(grad_two.astype(jnp.bfloat16), "mp", axis=0, tiled=True)
    grad_down_w = contract_rows(hidden, grad_two_all)
    grad_hidden = contract_cols(grad_two_all, down_full)
    grad_gate = (
        grad_hidden * up_act * sigmoid_gate * (1.0 + gate_act * (1.0 - sigmoid_gate))
    ).astype(jnp.bfloat16)
    grad_up = (grad_hidden * silu_gate).astype(jnp.bfloat16)
    grad_gate_w = contract_rows(middle_all, grad_gate)
    grad_up_w = contract_rows(middle_all, grad_up)
    grad_middle = grad_two + lax.psum_scatter(
        contract_cols(grad_gate, gate_full) + contract_cols(grad_up, up_full),
        "mp",
        scatter_dimension=0,
        tiled=True,
    )
    grad_one, first_gain_part, first_bias_part = norm_back(
        grad_middle, first_hat, first_inv, gain_one
    )
    grad_one_all = lax.all_gather(grad_one.astype(jnp.bfloat16), "mp", axis=0, tiled=True)
    grad_out_w = contract_rows(merged, grad_one_all)
    grad_merged = contract_cols(grad_one_all, out_full).astype(jnp.bfloat16)
    query_grad, key_grad, value_grad = attend_backward(
        queries,
        key_rot,
        values,
        seg_rows,
        local_heads,
        score_scale,
        row_max,
        row_sum,
        to_heads(grad_merged),
    )
    query_pre = from_heads(rotate(query_grad, cos_table, -sin_table).astype(jnp.bfloat16))
    key_pre = from_heads(rotate(key_grad, cos_table, -sin_table).astype(jnp.bfloat16))
    value_pre = from_heads(value_grad.astype(jnp.bfloat16))
    stacked = jnp.stack([query_pre, key_pre, value_pre])
    grad_qkv_w = jnp.einsum("sd,ksc->kdc", rows_all, stacked, preferred_element_type=jnp.float32)
    grad_inputs = grad_one + lax.psum_scatter(
        jnp.einsum("ksc,kdc->sd", stacked, qkv_full, preferred_element_type=jnp.float32).astype(
            jnp.bfloat16
        ),
        "mp",
        scatter_dimension=0,
        tiled=True,
    ).astype(jnp.float32)
    reduced = tuple(
        (
            lax.psum_scatter(grad_qkv_w, "dp", scatter_dimension=1, tiled=True),
            lax.psum_scatter(grad_out_w, "dp", scatter_dimension=1, tiled=True),
            lax.psum_scatter(first_gain_part, "dp", scatter_dimension=0, tiled=True),
            lax.psum_scatter(first_bias_part, "dp", scatter_dimension=0, tiled=True),
            lax.psum_scatter(grad_gate_w, "dp", scatter_dimension=0, tiled=True),
            lax.psum_scatter(grad_up_w, "dp", scatter_dimension=0, tiled=True),
            lax.psum_scatter(grad_down_w, "dp", scatter_dimension=1, tiled=True),
            lax.psum_scatter(second_gain_part, "dp", scatter_dimension=0, tiled=True),
            lax.psum_scatter(second_bias_part, "dp", scatter_dimension=0, tiled=True),
        )
    )
    norm_sums = lax.psum((reduced[2], reduced[3], reduced[7], reduced[8]), "mp")
    return (
        outputs,
        grad_inputs,
        reduced[0],
        reduced[1],
        norm_sums[0],
        norm_sums[1],
        reduced[4],
        reduced[5],
        reduced[6],
        norm_sums[2],
        norm_sums[3],
    )


def solution(mesh):
    return jax.shard_map(
        on_device,
        mesh=mesh,
        in_specs=(
            P(("dp", "mp"), None),
            P("dp"),
            P(None, "dp", "mp"),
            P("mp", "dp"),
            P("dp"),
            P("dp"),
            P("dp", "mp"),
            P("dp", "mp"),
            P("mp", "dp"),
            P("dp"),
            P("dp"),
            P(("dp", "mp"), None),
        ),
        out_specs=(
            P(("dp", "mp"), None),
            P(("dp", "mp"), None),
            P(None, "dp", "mp"),
            P("mp", "dp"),
            P("dp"),
            P("dp"),
            P("dp", "mp"),
            P("dp", "mp"),
            P("mp", "dp"),
            P("dp"),
            P("dp"),
        ),
        check_vma=False,
    )
```

profile of v0, /device:TPU:0, one launch (start us, length us, event | category | flops | bytes accessed | tf_op | source)
XLA Modules:
  0.0 1790.4 jit_solution(16121359778143721087)
XLA Ops:
  11.2 26.1 %all_gather.41 = bf16[384,768]{0,1:T(8,128)(2,1)} all-gather(bf16[384,48]{0,1:T(8,128)(2,1)S(1)} %copy-done.19), channel_id=1, replica_groups=mesh['dp'=16,'mp'=2] {'dp'}, dimensions={1}, use_global_device_ids=true | all-gather | bytes 626688 | tf_op jit(solution)/shard_map/all_gather | solution.py:167
  57.2 42.7 %all-gather.9.cloned.1.call-done = bf16[3,768,384]{2,1,0:T(8,128)(2,1)} async-done(((bf16[3,48,384]{2,1,0:T(8,128)(2,1)}), bf16[3,768,384]{2,1,0:T(8,128)(2,1)}) %all-gather.9.cloned.1.call-update) | async-done | bytes 1769488 | tf_op jit(solution)/shard_map/all_gather | solution.py:166
  119.4 202.3 %while.64 = (s32[]{:T(128)}, bf16[6,2048,64]{1,2,0:T(8,128)(2,1)}, f32[6,2048]{1,0:T(8,128)S(1)}, f32[6,2048]{1,0:T(8,128)}, s32[6]{0:T(128)S(1)}, /*index=5*/bf...) while((s32[]{:T(128)}, bf16[6,2048,64]{1,2,0:T(8,128)(2,1)}, ...), condition=%wide.region_5.6_spmd.clone, body=%wide.region_0.5_spmd.sunk.clone | while | flops 285212672 | bytes 17165348 | solution.py:101
  124.4 25.8 %while.63 = (s32[]{:T(128)}, bf16[4,512,64]{1,2,0:T(8,128)(2,1)S(1)}, f32[4,512]{1,0:T(4,128)S(1)}, f32[4,512]{1,0:T(4,128)S(1)}, s32[4]{0:T(128)S(1)}, /*index=...) while((s32[]{:T(128)}, ...), condition=%wide.region_4.4_spmd, body=%wide.region_1.3_spmd.sunk | while | flops 285212672 | bytes 13953235 | solution.py:98
  158.1 25.8 %while.63 = (s32[]{:T(128)}, bf16[4,512,64]{1,2,0:T(8,128)(2,1)S(1)}, f32[4,512]{1,0:T(4,128)S(1)}, f32[4,512]{1,0:T(4,128)S(1)}, s32[4]{0:T(128)S(1)}, /*index=...) while((s32[]{:T(128)}, ...), condition=%wide.region_4.4_spmd, body=%wide.region_1.3_spmd.sunk | while | flops 285212672 | bytes 13953235 | solution.py:98
  191.7 25.8 %while.63 = (s32[]{:T(128)}, bf16[4,512,64]{1,2,0:T(8,128)(2,1)S(1)}, f32[4,512]{1,0:T(4,128)S(1)}, f32[4,512]{1,0:T(4,128)S(1)}, s32[4]{0:T(128)S(1)}, /*index=...) while((s32[]{:T(128)}, ...), condition=%wide.region_4.4_spmd, body=%wide.region_1.3_spmd.sunk | while | flops 285212672 | bytes 13953235 | solution.py:98
  225.4 25.8 %while.63 = (s32[]{:T(128)}, bf16[4,512,64]{1,2,0:T(8,128)(2,1)S(1)}, f32[4,512]{1,0:T(4,128)S(1)}, f32[4,512]{1,0:T(4,128)S(1)}, s32[4]{0:T(128)S(1)}, /*index=...) while((s32[]{:T(128)}, ...), condition=%wide.region_4.4_spmd, body=%wide.region_1.3_spmd.sunk | while | flops 285212672 | bytes 13953235 | solution.py:98
  259.1 25.8 %while.63 = (s32[]{:T(128)}, bf16[4,512,64]{1,2,0:T(8,128)(2,1)S(1)}, f32[4,512]{1,0:T(4,128)S(1)}, f32[4,512]{1,0:T(4,128)S(1)}, s32[4]{0:T(128)S(1)}, /*index=...) while((s32[]{:T(128)}, ...), condition=%wide.region_4.4_spmd, body=%wide.region_1.3_spmd.sunk | while | flops 285212672 | bytes 13953235 | solution.py:98
  292.8 25.8 %while.63 = (s32[]{:T(128)}, bf16[4,512,64]{1,2,0:T(8,128)(2,1)S(1)}, f32[4,512]{1,0:T(4,128)S(1)}, f32[4,512]{1,0:T(4,128)S(1)}, s32[4]{0:T(128)S(1)}, /*index=...) while((s32[]{:T(128)}, ...), condition=%wide.region_4.4_spmd, body=%wide.region_1.3_spmd.sunk | while | flops 285212672 | bytes 13953235 | solution.py:98
  330.5 32.1 %all-reduce.11 = (bf16[768]{0:T(1024)(128)(2,1)S(1)}, bf16[768]{0:T(1024)(128)(2,1)S(1)}, bf16[768]{0:T(1024)(128)(2,1)S(1)}, bf16[768]{0:T(1024)(128)(2,1)S(1)}) all-reduce(bf16[768]{0:T(1024)(128)(2,1)S(1)} %dynamic-update-slice.1, bf16[768]{0:T(1024)(128)(2,1)S(1)} %dynamic-update-slice, ...), channel_id=1, replica_groups=mesh['dp'=16,'mp'=2] {'dp'}, use_global_device_ids=true, to_apply=%add.1 | all-reduce | flops 3072 | bytes 12288
  362.6 41.2 %reduce-scatter.9.cloned.1.call-done = f32[1024,768]{1,0:T(8,128)} async-done(((f32[2048,768]{1,0:T(8,128)}), f32[1024,768]{1,0:T(8,128)}) %reduce-scatter.9.cloned.1.call-update) | async-done | bytes 3145744 | tf_op jit(solution)/shard_map/reduce_scatter | solution.py:211
  410.1 38.4 %all-gather.15.cloned.1.call-done = bf16[768,1536]{1,0:T(8,128)(2,1)} async-done(((bf16[48,1536]{1,0:T(8,128)(2,1)}), bf16[768,1536]{1,0:T(8,128)(2,1)}) %all-gather.15.cloned.1.call-update) | async-done | bytes 2359312 | tf_op jit(solution)/shard_map/all_gather | solution.py:172
  448.6 45.8 %all-gather.13.cloned.1.call-done = bf16[2048,768]{1,0:T(8,128)(2,1)} async-done(((bf16[1024,768]{1,0:T(8,128)(2,1)}), bf16[2048,768]{1,0:T(8,128)(2,1)}) %all-gather.13.cloned.1.call-update) | async-done | bytes 3145744 | tf_op jit(solution)/shard_map/all_gather | solution.py:220
  504.3 34.8 %all-gather.17.cloned.1.call-done = bf16[768,1536]{1,0:T(8,128)(2,1)} async-done(((bf16[48,1536]{1,0:T(8,128)(2,1)}), bf16[768,1536]{1,0:T(8,128)(2,1)}) %all-gather.17.cloned.1.call-update) | async-done | bytes 2359312 | tf_op jit(solution)/shard_map/all_gather | solution.py:173
  553.1 29.7 %all-gather.19.cloned.1.call-done = bf16[1536,768]{0,1:T(8,128)(2,1)} async-done(((bf16[1536,48]{0,1:T(8,128)(2,1)}), bf16[1536,768]{0,1:T(8,128)(2,1)}) %all-gather.19.cloned.1.call-update) | async-done | bytes 2359312 | tf_op jit(solution)/shard_map/all_gather | solution.py:174
  592.5 75.9 %reduce-scatter.11.cloned.1.call-done = f32[1024,768]{1,0:T(8,128)} async-done(((f32[2048,768]{1,0:T(8,128)}), f32[1024,768]{1,0:T(8,128)}) %reduce-scatter.11.cloned.1.call-update) | async-done | bytes 3145744 | tf_op jit(solution)/shard_map/reduce_scatter | solution.py:226
  678.6 45.0 %all-gather.21.cloned.1.call-done = bf16[2048,768]{1,0:T(8,128)(2,1)} async-done(((bf16[1024,768]{1,0:T(8,128)(2,1)}), bf16[2048,768]{1,0:T(8,128)(2,1)}) %all-gather.21.cloned.1.call-update) | async-done | bytes 3145744 | tf_op jit(solution)/shard_map/all_gather | solution.py:237
  757.6 77.1 %reduce-scatter.13.cloned.1.call-done = f32[1024,768]{1,0:T(8,128)} async-done(((f32[2048,768]{1,0:T(8,128)}), f32[1024,768]{1,0:T(8,128)}) %reduce-scatter.13.cloned.1.call-update) | async-done | bytes 3145744 | tf_op jit(solution)/shard_map/reduce_scatter | solution.py:246
  843.9 45.0 %all-gather.23.cloned.1.call-done = bf16[2048,768]{1,0:T(8,128)(2,1)} async-done(((bf16[1024,768]{1,0:T(8,128)(2,1)}), bf16[2048,768]{1,0:T(8,128)(2,1)}) %all-gather.23.cloned.1.call-update) | async-done | bytes 3145744 | tf_op jit(solution)/shard_map/all_gather | solution.py:255
  897.4 399.8 %while.66 = (s32[]{:T(128)}, f32[6,2048,64]{1,2,0:T(8,128)}, f32[6,2048,64]{1,2,0:T(8,128)}, bf16[6,2048,64]{1,2,0:T(8,128)(2,1)}, s32[6]{0:T(128)S(1)}, /*index...) while((s32[]{:T(128)}, f32[6,2048,64]{1,2,0:T(8,128)}, ...), condition=%wide.region_21.22_spmd.clone, body=%wide.region_17.21_spmd.sunk.clone | while | flops 685408768 | bytes 83035496 | solution.py:148
  905.2 54.3 %while.65 = (s32[]{:T(128)}, f32[2048,64]{0,1:T(8,128)}, f32[2048,64]{0,1:T(8,128)S(1)}, f32[4,512,64]{1,2,0:T(8,128)}, s32[4]{0:T(128)S(1)}, /*index=5*/s32[204...) while((s32[]{:T(128)}, f32[2048,64]{0,1:T(8,128)}, ...), condition=%wide.region_20.20_spmd.clone, body=%wide.region_18.19_spmd.clone.sunk | while | flops 685408768 | bytes 75661288 | solution.py:143
  971.8 54.2 %while.65 = (s32[]{:T(128)}, f32[2048,64]{0,1:T(8,128)}, f32[2048,64]{0,1:T(8,128)S(1)}, f32[4,512,64]{1,2,0:T(8,128)}, s32[4]{0:T(128)S(1)}, /*index=5*/s32[204...) while((s32[]{:T(128)}, f32[2048,64]{0,1:T(8,128)}, ...), condition=%wide.region_20.20_spmd.clone, body=%wide.region_18.19_spmd.clone.sunk | while | flops 685408768 | bytes 75661288 | solution.py:143
  1038.4 54.3 %while.65 = (s32[]{:T(128)}, f32[2048,64]{0,1:T(8,128)}, f32[2048,64]{0,1:T(8,128)S(1)}, f32[4,512,64]{1,2,0:T(8,128)}, s32[4]{0:T(128)S(1)}, /*index=5*/s32[204...) while((s32[]{:T(128)}, f32[2048,64]{0,1:T(8,128)}, ...), condition=%wide.region_20.20_spmd.clone, body=%wide.region_18.19_spmd.clone.sunk | while | flops 685408768 | bytes 75661288 | solution.py:143
  1105.1 54.2 %while.65 = (s32[]{:T(128)}, f32[2048,64]{0,1:T(8,128)}, f32[2048,64]{0,1:T(8,128)S(1)}, f32[4,512,64]{1,2,0:T(8,128)}, s32[4]{0:T(128)S(1)}, /*index=5*/s32[204...) while((s32[]{:T(128)}, f32[2048,64]{0,1:T(8,128)}, ...), condition=%wide.region_20.20_spmd.clone, body=%wide.region_18.19_spmd.clone.sunk | while | flops 685408768 | bytes 75661288 | solution.py:143
  1171.7 54.2 %while.65 = (s32[]{:T(128)}, f32[2048,64]{0,1:T(8,128)}, f32[2048,64]{0,1:T(8,128)S(1)}, f32[4,512,64]{1,2,0:T(8,128)}, s32[4]{0:T(128)S(1)}, /*index=5*/s32[204...) while((s32[]{:T(128)}, f32[2048,64]{0,1:T(8,128)}, ...), condition=%wide.region_20.20_spmd.clone, body=%wide.region_18.19_spmd.clone.sunk | while | flops 685408768 | bytes 75661288 | solution.py:143
  1238.3 54.2 %while.65 = (s32[]{:T(128)}, f32[2048,64]{0,1:T(8,128)}, f32[2048,64]{0,1:T(8,128)S(1)}, f32[4,512,64]{1,2,0:T(8,128)}, s32[4]{0:T(128)S(1)}, /*index=5*/s32[204...) while((s32[]{:T(128)}, f32[2048,64]{0,1:T(8,128)}, ...), condition=%wide.region_20.20_spmd.clone, body=%wide.region_18.19_spmd.clone.sunk | while | flops 685408768 | bytes 75661288 | solution.py:143
  1369.3 62.3 %all-reduce.9 = (f32[768]{0:T(1024)S(1)}, f32[768]{0:T(1024)S(1)}, f32[768]{0:T(1024)S(1)}, f32[768]{0:T(1024)S(1)}) all-reduce(f32[768]{0:T(1024)S(1)} %copy-done.20, f32[768]{0:T(1024)S(1)} %copy-done.21, f32[768]{0:T(1024)S(1)} %copy-done.22, f32[768]{0:T(1024)S(1)} %copy-done.23), channel_id=8, replica_groups=mesh['dp'=16,'mp'=2] {'dp'}, use_global_device_ids=true, to_apply=%region_26.27.clone | all-reduce | flops 3072 | bytes 24576
  1439.4 44.3 %reduce-scatter.15.cloned.1.call-done = bf16[1024,768]{1,0:T(8,128)(2,1)} async-done(((bf16[2048,768]{1,0:T(8,128)(2,1)}), bf16[1024,768]{1,0:T(8,128)(2,1)}) %reduce-scatter.15.cloned.1.call-update) | async-done | bytes 1572880 | tf_op jit(solution)/shard_map/reduce_scatter | solution.py:274
  1487.1 76.5 %reduce-scatter.23.cloned.1.call-done = f32[1536,48]{0,1:T(8,128)} async-done(((f32[1536,768]{0,1:T(8,128)}), f32[1536,48]{0,1:T(8,128)}) %reduce-scatter.23.cloned.1.call-update) | async-done | bytes 294928 | tf_op jit(solution)/shard_map/reduce_scatter | solution.py:290
  1563.6 79.4 %reduce-scatter.19.cloned.1.call-done = f32[48,1536]{1,0:T(8,128)} async-done(((f32[768,1536]{1,0:T(8,128)}), f32[48,1536]{1,0:T(8,128)}) %reduce-scatter.19.cloned.1.call-update) | async-done | bytes 294928 | tf_op jit(solution)/shard_map/reduce_scatter | solution.py:288
  1643.0 78.9 %reduce-scatter.21.cloned.1.call-done = f32[48,1536]{1,0:T(8,128)} async-done(((f32[768,1536]{1,0:T(8,128)}), f32[48,1536]{1,0:T(8,128)}) %reduce-scatter.21.cloned.1.call-update) | async-done | bytes 294928 | tf_op jit(solution)/shard_map/reduce_scatter | solution.py:289
  1721.9 61.6 %reduce-scatter.17.cloned.1.call-done = f32[384,48]{0,1:T(8,128)} async-done(((f32[384,768]{0,1:T(8,128)}), f32[384,48]{0,1:T(8,128)}) %reduce-scatter.17.cloned.1.call-update) | async-done | bytes 73744 | tf_op jit(solution)/shard_map/reduce_scatter | solution.py:285
  (1156 shorter events, 777.5 us)
Async XLA Ops:
  7.2 50.0 %all-gather.11.cloned.1.call-start = ((), (), s32[]{:S(2)}) async-start(), calls=%async_computation.9 | async-start | bytes 4718592 | tf_op jit(solution)/shard_map/all_gather | solution.py:184
  7.9 92.1 %all-gather.9.cloned.1.call-start = ((), (), s32[]{:S(2)}) async-start(), calls=%async_computation.8 | async-start | bytes 1880064 | tf_op jit(solution)/shard_map/all_gather | solution.py:166
  8.7 395.1 %reduce-scatter.9.cloned.1.call-start = ((), (), s32[]{:S(2)}) async-start(), calls=%async_computation.10 | async-start | bytes 9437184 | tf_op jit(solution)/shard_map/reduce_scatter | solution.py:211
  39.2 68.2 %copy-start.15 = (f32[2048,32]{0,1:T(8,128)}, f32[2048,32]{0,1:T(8,128)S(1)}, u32[]{:S(2)}) copy-start(f32[2048,32]{0,1:T(8,128)S(1)} %get-tuple-element.541) | copy-start | bytes 786436
  119.4 202.3 %copy-start.14 = (bf16[384,768]{0,1:T(8,128)(2,1)S(1)}, bf16[384,768]{0,1:T(8,128)(2,1)}, u32[]{:S(2)}) copy-start(bf16[384,768]{0,1:T(8,128)(2,1)} %all_gather.41) | copy-start | bytes 1769476
  327.7 120.9 %all-gather.15.cloned.1.call-start = ((), (), s32[]{:S(2)}) async-start(), calls=%async_computation.12 | async-start | bytes 2506752 | tf_op jit(solution)/shard_map/all_gather | solution.py:172
  328.3 166.1 %all-gather.13.cloned.1.call-start = ((), (), s32[]{:S(2)}) async-start(), calls=%async_computation.11 | async-start | bytes 4718592 | tf_op jit(solution)/shard_map/all_gather | solution.py:220
  408.8 130.3 %all-gather.17.cloned.1.call-start = ((), (), s32[]{:S(2)}) async-start(), calls=%async_computation.13 | async-start | bytes 2506752 | tf_op jit(solution)/shard_map/all_gather | solution.py:173
  409.3 173.4 %all-gather.19.cloned.1.call-start = ((), (), s32[]{:S(2)}) async-start(), calls=%async_computation.14 | async-start | bytes 2506752 | tf_op jit(solution)/shard_map/all_gather | solution.py:174
  410.1 258.3 %reduce-scatter.11.cloned.1.call-start = ((), (), s32[]{:S(2)}) async-start(), calls=%async_computation.15 | async-start | bytes 9437184 | tf_op jit(solution)/shard_map/reduce_scatter | solution.py:226
  592.4 131.2 %all-gather.21.cloned.1.call-start = ((), (), s32[]{:S(2)}) async-start(), calls=%async_computation.16 | async-start | bytes 4718592 | tf_op jit(solution)/shard_map/all_gather | solution.py:237
  671.2 5.3 copy-start.6
  678.5 156.2 %reduce-scatter.13.cloned.1.call-start = ((), (), s32[]{:S(2)}) async-start(), calls=%async_computation.17 | async-start | bytes 9437184 | tf_op jit(solution)/shard_map/reduce_scatter | solution.py:246
  723.6 19.6 %copy-start.27 = (bf16[768,1536]{1,0:T(8,128)(2,1)S(1)}, bf16[768,1536]{1,0:T(8,128)(2,1)}, u32[]{:S(2)}) copy-start(bf16[768,1536]{1,0:T(8,128)(2,1)} %all-gather.15.cloned.1.call-done) | copy-start | bytes 7077892
  743.2 7.4 copy-start.28
  743.2 7.4 copy-start.33
  757.5 131.4 %all-gather.23.cloned.1.call-start = ((), (), s32[]{:S(2)}) async-start(), calls=%async_computation.18 | async-start | bytes 4718592 | tf_op jit(solution)/shard_map/all_gather | solution.py:255
  843.8 593.9 %all-reduce.14.cloned.1.call-start = ((), (), s32[]{:S(2)}) async-start(), calls=%async_computation.24 | async-start | bytes 9437184
  897.4 399.8 %copy-start.16 = (f32[2048,32]{0,1:T(8,128)S(1)}, f32[2048,32]{0,1:T(8,128)}, u32[]{:S(2)}) copy-start(f32[2048,32]{0,1:T(8,128)} %copy-done.15) | copy-start | bytes 786436
  925.5 5.1 copy-start.1
  1058.8 5.1 copy-start.1
  1192.0 5.1 copy-start.1
  1320.3 163.5 %reduce-scatter.15.cloned.1.call-start = ((), (), s32[]{:S(2)}) async-start(), calls=%async_computation.19 | async-start | bytes 4718592 | tf_op jit(solution)/shard_map/reduce_scatter | solution.py:274
  1330.1 233.4 %reduce-scatter.23.cloned.1.call-start = ((), (), s32[]{:S(2)}) async-start(), calls=%async_computation.23 | async-start | bytes 5013504 | tf_op jit(solution)/shard_map/reduce_scatter | solution.py:290
  1341.8 301.2 %reduce-scatter.19.cloned.1.call-start = ((), (), s32[]{:S(2)}) async-start(), calls=%async_computation.21 | async-start | bytes 5013504 | tf_op jit(solution)/shard_map/reduce_scatter | solution.py:288
  1353.3 368.6 %reduce-scatter.21.cloned.1.call-start = ((), (), s32[]{:S(2)}) async-start(), calls=%async_computation.22 | async-start | bytes 5013504 | tf_op jit(solution)/shard_map/reduce_scatter | solution.py:289
  1363.0 6.3 copy-start.20
  1363.0 6.3 copy-start.21
  1363.1 6.3 copy-start.22
  1363.1 6.3 copy-start.23
  1363.1 420.5 %reduce-scatter.17.cloned.1.call-start = ((), (), s32[]{:S(2)}) async-start(), calls=%async_computation.20 | async-start | bytes 1253376 | tf_op jit(solution)/shard_map/reduce_scatter | solution.py:285
  1363.1 120.6 %copy-start.12 = (f32[1024,768]{1,0:T(8,128)S(1)}, f32[1024,768]{1,0:T(8,128)}, u32[]{:S(2)}) copy-start(f32[1024,768]{1,0:T(8,128)} %get-tuple-element.504) | copy-start | bytes 9437188
  (203 other events, 621.1 us)
Sparse Core Ops, SparseCore 0:
  9.6 47.6 all-gather.10
  59.5 40.3 all-gather.8
  327.8 75.9 reduce-scatter.8
  406.2 42.3 all-gather.14
  450.6 43.7 all-gather.12
  496.8 42.3 all-gather.16
  541.7 41.0 all-gather.18
  592.5 75.8 reduce-scatter.10
  678.7 44.9 all-gather.20
  757.7 77.0 reduce-scatter.12
  843.9 44.9 all-gather.22
  1320.4 117.2 all-reduce.13
  1440.6 43.0 reduce-scatter.14
  1488.0 75.5 reduce-scatter.22
  1568.3 74.5 reduce-scatter.18
  1647.3 74.5 reduce-scatter.20
  1726.4 57.1 reduce-scatter.16
where the time goes:
time: 1800 us; the launch traced here: 1790 us
  waiting for transfers between devices  838 us (47%)
  matrix products  438 us (24%)
  local copies, waits for them, and re-layouts  218 us (12%)
  blocking collectives  126 us (7%)
  other arithmetic  93.3 us (5%)
  loops' own time  60 us (3%)
    dot_general x76, matrix products, contract_cols(): lax.dot_general(left_op, right_op, (((1,), (1,)), ((), ())), preferred_el...  135 us
    dot_general x52, matrix products, contract_rows(): lax.dot_general(left_op, right_op, (((0,), (0,)), ((), ())), preferred_el...  134 us
    unnamed x2, blocking collectives  94.3 us
    reduce_scatter x1, waiting for transfers between devices, on_device(): lax.psum_scatter(grad_gate_w, 'dp', scatter_dimension=0, tiled=True)  79.4 us
    reduce_scatter x1, waiting for transfers between devices, on_device(): lax.psum_scatter(grad_up_w, 'dp', scatter_dimension=0, tiled=True)  78.9 us
    reduce_scatter x1, waiting for transfers between devices, on_device(): lax.psum_scatter(contract_cols(grad_gate, gate_full) + contract_cols(grad...  77.1 us
    reduce_scatter x1, waiting for transfers between devices, on_device(): lax.psum_scatter(grad_down_w, 'dp', scatter_dimension=1, tiled=True)  76.5 us
    reduce_scatter x1, waiting for transfers between devices, on_device(): lax.psum_scatter(jnp.dot(hidden, down_full, preferred_element_type=jnp.fl...  75.9 us
  transfers between devices with their start and end apart: 17, of which 17 were waited for; matrix products, arithmetic and copies ran while one was open for 5% of the time, Pallas kernels for 0%

commit v1 on v0

v1 whole, which is shorter than its diff:
```python
import functools

import jax
import jax.numpy as jnp
import numpy as np
from jax import lax
from jax.experimental import pallas as pl
from jax.experimental.pallas import tpu as pltpu
from jax.sharding import Mesh
from jax.sharding import PartitionSpec as P

HEAD_DIM = 64
SEQ_LEN = 2048
LANES = 128
EPSILON = 1e-12
ROPE_BASE = 1000.0
MASKED = -10000.0
SCALE = HEAD_DIM**-0.5
F32 = jnp.float32
BF16 = jnp.bfloat16
NT = (((1,), (1,)), ((), ()))
NN = (((1,), (0,)), ((), ()))
TN = (((0,), (0,)), ((), ()))
VMEM_BYTES = 56 << 20
FWD_Q, FWD_K = 1024, 512
BWD_Q, BWD_K = 1024, 512
ROW_BLOCK = 256


def dot(left, right, dims=NN):
    return lax.dot_general(left, right, dims, preferred_element_type=F32)


def rope_tables():
    half = HEAD_DIM // 2
    frequency = ROPE_BASE ** (-2.0 * np.arange(half) / HEAD_DIM)
    angles = np.arange(SEQ_LEN)[:, None] * frequency[None, :]
    cos, sin = np.cos(angles), np.sin(angles)
    heads = LANES // HEAD_DIM
    return (
        np.tile(np.concatenate([cos, cos], 1), (1, heads)).astype(np.float32),
        np.tile(np.concatenate([-sin, sin], 1), (1, heads)).astype(np.float32),
    )


def half_swap(tile):
    lane = lax.broadcasted_iota(jnp.int32, (1, LANES), 1)
    half = HEAD_DIM // 2
    return jnp.where(
        lane % HEAD_DIM < half,
        pltpu.roll(tile, LANES - half, 1),
        pltpu.roll(tile, half, 1),
    )


def project_kernel(core_ref, x_ref, w_ref, cos_ref, sin_ref, out_ref, *, pairs):
    x = x_ref[...]
    cos, sin = cos_ref[...], sin_ref[...]
    for pair in range(pairs):
        base = pair * 3 * LANES
        tile = dot(x, w_ref[:, base : base + 3 * LANES])
        for kind in range(2):
            part = tile[:, kind * LANES : (kind + 1) * LANES]
            out_ref[:, base + kind * LANES : base + (kind + 1) * LANES] = (
                part * cos + half_swap(part) * sin
            ).astype(BF16)
        out_ref[:, base + 2 * LANES : base + 3 * LANES] = tile[:, 2 * LANES :].astype(BF16)


def project(core, rows, weights, cos, sin):
    tokens, depth = rows.shape
    wide = weights.shape[1]
    steps = tokens // ROW_BLOCK

    def turned(step, core_ref):
        return (lax.rem(step + core_ref[0] * (steps // 2), steps), 0)

    return pl.pallas_call(
        functools.partial(project_kernel, pairs=wide // (3 * LANES)),
        grid_spec=pltpu.PrefetchScalarGridSpec(
            num_scalar_prefetch=1,
            grid=(steps,),
            in_specs=[
                pl.BlockSpec((ROW_BLOCK, depth), lambda i, c: (i, 0)),
                pl.BlockSpec((depth, wide), lambda i, c: (0, 0)),
                pl.BlockSpec((ROW_BLOCK, LANES), turned),
                pl.BlockSpec((ROW_BLOCK, LANES), turned),
            ],
            out_specs=pl.BlockSpec((ROW_BLOCK, wide), lambda i, c: (i, 0)),
        ),
        out_shape=jax.ShapeDtypeStruct((tokens, wide), BF16),
        compiler_params=pltpu.CompilerParams(vmem_limit_bytes=VMEM_BYTES),
        cost_estimate=pl.CostEstimate(
            flops=2 * tokens * depth * wide,
            bytes_accessed=2 * tokens * (depth + wide) + 2 * depth * wide,
            transcendentals=0,
        ),
        name="project",
    )(core, rows, weights, cos, sin)


def block_range(labels, block, other, turn):
    blocks = labels.shape[0] // block
    valid = labels >= 0
    tiles = labels.reshape(blocks, block)
    first, last = tiles[:, 0], jnp.max(tiles, axis=1)
    low = jnp.sum((valid[None] & (labels[None] < first[:, None])).astype(jnp.int32), 1)
    high = jnp.sum((valid[None] & (labels[None] <= last[:, None])).astype(jnp.int32), 1)
    offset = (labels.shape[0] - turn) // other
    return low // other + offset, jnp.where(high > low, (high + other - 1) // other, low // other) + offset


def attend_kernel(low_ref, high_ref, q_ref, k_ref, v_ref, key_ref, query_ref, o_ref, lse_ref, v_turned):
    tokens = q_ref.shape[0]
    key_blocks = tokens // FWD_K
    lane = lax.broadcasted_iota(jnp.int32, (1, LANES), 1)
    zero = jnp.zeros((), BF16)
    v_turned[...] = v_ref[...].T

    @pl.loop(0, tokens // FWD_Q)
    def _(i):
        q0 = pl.multiple_of(i * FWD_Q, FWD_Q)
        scaled = q_ref[pl.ds(q0, FWD_Q), :] * jnp.asarray(SCALE, BF16)
        halves = (
            jnp.where(lane < HEAD_DIM, scaled, zero),
            jnp.where(lane >= HEAD_DIM, scaled, zero),
        )
        query_label = query_ref[:, pl.ds(q0, FWD_Q)]

        def body(j, carry):
            k0 = pl.multiple_of(lax.rem(j, key_blocks) * FWD_K, FWD_K)
            k = k_ref[pl.ds(k0, FWD_K), :]
            same = key_ref[pl.ds(k0, FWD_K), :] == query_label
            scores = [dot(k, half, NT) for half in halves]
            out = []
            for h in range(2):
                top, total, acc = carry[h]
                s = jnp.where(same, scores[h], -1e30)
                new_top = jnp.maximum(top, jnp.max(s, axis=0, keepdims=True))
                fade = jnp.exp(top - new_top)
                e = jnp.exp(s - new_top)
                total = fade * total + jnp.sum(e, axis=0, keepdims=True)
                part = dot(v_turned[h * HEAD_DIM : (h + 1) * HEAD_DIM, pl.ds(k0, FWD_K)], e.astype(BF16))
                out.append((new_top, total, acc * fade + part))
            return tuple(out)

        start = (
            jnp.full((1, FWD_Q), MASKED, F32),
            jnp.zeros((1, FWD_Q), F32),
            jnp.zeros((HEAD_DIM, FWD_Q), F32),
        )
        ended = lax.fori_loop(low_ref[i], high_ref[i], body, (start, start))
        out = []
        for h in range(2):
            top, total, acc = ended[h]
            norm = jnp.maximum(total, 1.0)
            out.append(acc / norm)
            lse_ref[0, pl.ds(h, 1), pl.ds(q0, FWD_Q)] = top + jnp.log(norm)
        o_ref[pl.ds(q0, FWD_Q), :] = jnp.concatenate(out, 0).T.astype(BF16)


def attend(qkv, labels, turn):
    tokens = qkv.shape[0]
    pairs = qkv.shape[1] // (3 * LANES)
    low, high = block_range(labels, FWD_Q, FWD_K, turn)
    queries = jnp.where(labels < 0, -2, labels)
    whole = lambda shape: pl.BlockSpec(shape, lambda p, *_: (0,) * len(shape))
    part = lambda kind: pl.BlockSpec((tokens, LANES), lambda p, *_: (0, 3 * p + kind))
    return pl.pallas_call(
        attend_kernel,
        grid_spec=pltpu.PrefetchScalarGridSpec(
            num_scalar_prefetch=2,
            grid=(pairs,),
            in_specs=[part(0), part(1), part(2), whole((tokens, 1)), whole((1, tokens))],
            out_specs=[
                pl.BlockSpec((tokens, LANES), lambda p, *_: (0, p)),
                pl.BlockSpec((1, 2, tokens), lambda p, *_: (p, 0, 0)),
            ],
            scratch_shapes=[pltpu.VMEM((LANES, tokens), BF16)],
        ),
        out_shape=[
            jax.ShapeDtypeStruct((tokens, pairs * LANES), BF16),
            jax.ShapeDtypeStruct((pairs, 2, tokens), F32),
        ],
        compiler_params=pltpu.CompilerParams(vmem_limit_bytes=VMEM_BYTES),
        cost_estimate=pl.CostEstimate(
            flops=pairs * 8 * tokens * tokens * LANES,
            bytes_accessed=pairs * 4 * tokens * LANES * 2,
            transcendentals=pairs * 2 * tokens * tokens,
        ),
        name="attend",
    )(low, high, qkv, qkv, qkv, labels[:, None], queries[None])


def attend_back_kernel(
    low_ref,
    high_ref,
    q_ref,
    k_ref,
    v_ref,
    o_ref,
    do_ref,
    lse_ref,
    key_ref,
    query_ref,
    cos_ref,
    sin_ref,
    out_ref,
    dq_turned,
    inner,
    k_turned,
    *,
    turn_steps,
):
    tokens = q_ref.shape[0]
    query_blocks = tokens // BWD_Q
    lane = lax.broadcasted_iota(jnp.int32, (1, LANES), 1)
    zero = jnp.zeros((), BF16)
    picks = (lane < HEAD_DIM, lane >= HEAD_DIM)
    k_turned[...] = k_ref[...].T
    product = (o_ref[...].astype(F32) * do_ref[...].astype(F32)).T
    inner[0:1, :] = jnp.sum(product[:HEAD_DIM], axis=0, keepdims=True)
    inner[1:2, :] = jnp.sum(product[HEAD_DIM:], axis=0, keepdims=True)
    dq_turned[...] = jnp.zeros_like(dq_turned)

    def unrope(tile, row0, rows):
        cos, sin = cos_ref[pl.ds(row0, rows), :], sin_ref[pl.ds(row0, rows), :]
        return (tile * cos - half_swap(tile) * sin).astype(BF16)

    @pl.loop(0, tokens // BWD_K)
    def _(j):
        k0 = pl.multiple_of(j * BWD_K, BWD_K)
        key_label = key_ref[pl.ds(k0, BWD_K), :]
        dks, dvs = [], []
        for h in range(2):
            k = jnp.where(picks[h], k_ref[pl.ds(k0, BWD_K), :], zero)
            v = jnp.where(picks[h], v_ref[pl.ds(k0, BWD_K), :], zero)
            kt = k_turned[pl.ds(h * HEAD_DIM, HEAD_DIM), pl.ds(k0, BWD_K)]

            def body(i, carry):
                dk, dv = carry
                q0 = pl.multiple_of(lax.rem(i, query_blocks) * BWD_Q, BWD_Q)
                q = q_ref[pl.ds(q0, BWD_Q), :]
                do = do_ref[pl.ds(q0, BWD_Q), :]
                s = dot(k, q, NT)
                p = jnp.exp(s * SCALE - lse_ref[0, pl.ds(h, 1), pl.ds(q0, BWD_Q)])
                p = jnp.where(key_label == query_ref[:, pl.ds(q0, BWD_Q)], p, 0.0)
                dp = dot(v, do, NT)
                ds = (p * (dp - inner[pl.ds(h, 1), pl.ds(q0, BWD_Q)])).astype(BF16)
                dv = dv + dot(p.astype(BF16), do)
                dk = dk + dot(ds, q)
                dq_turned[pl.ds(h * HEAD_DIM, HEAD_DIM), pl.ds(q0, BWD_Q)] += dot(kt, ds)
                return dk, dv

            empty = jnp.zeros((BWD_K, LANES), F32)
            dk, dv = lax.fori_loop(low_ref[j], high_ref[j], body, (empty, empty))
            dks.append(dk)
            dvs.append(dv)
        dk = jnp.where(picks[0], dks[0], dks[1]) * SCALE
        out_ref[pl.ds(k0, BWD_K), LANES : 2 * LANES] = unrope(dk, k0, BWD_K)
        out_ref[pl.ds(k0, BWD_K), 2 * LANES :] = jnp.where(picks[0], dvs[0], dvs[1]).astype(BF16)

    out_ref[:, :LANES] = unrope(dq_turned[...].T * SCALE, 0, tokens)


def attend_back(pair, qkv, o, do, lse, labels, turn, cos, sin):
    tokens = qkv.shape[0]
    low, high = block_range(labels, BWD_K, BWD_Q, turn)
    queries = jnp.where(labels < 0, -2, labels)
    whole = lambda shape: pl.BlockSpec(shape, lambda g, *_: (0,) * len(shape))
    part = lambda kind: pl.BlockSpec((tokens, LANES), lambda g, *_: (0, 3 * pair + kind))
    own = pl.BlockSpec((tokens, LANES), lambda g, *_: (0, pair))
    return pl.pallas_call(
        functools.partial(attend_back_kernel, turn_steps=0),
        grid_spec=pltpu.PrefetchScalarGridSpec(
            num_scalar_prefetch=2,
            grid=(1,),
            in_specs=[
                part(0),
                part(1),
                part(2),
                own,
                own,
                pl.BlockSpec((1, 2, tokens), lambda g, *_: (pair, 0, 0)),
                whole((tokens, 1)),
                whole((1, tokens)),
                whole((tokens, LANES)),
                whole((tokens, LANES)),
            ],
            out_specs=whole((tokens, 3 * LANES)),
            scratch_shapes=[
                pltpu.VMEM((LANES, tokens), F32),
                pltpu.VMEM((8, tokens), F32),
                pltpu.VMEM((LANES, tokens), BF16),
            ],
        ),
        out_shape=jax.ShapeDtypeStruct((tokens, 3 * LANES), BF16),
        compiler_params=pltpu.CompilerParams(vmem_limit_bytes=VMEM_BYTES),
        cost_estimate=pl.CostEstimate(
            flops=20 * tokens * tokens * LANES,
            bytes_accessed=8 * tokens * LANES * 2,
            transcendentals=2 * tokens * tokens,
        ),
        name="attend_back",
    )(low, high, qkv, qkv, qkv, o, do, lse, labels[:, None], queries[None], cos, sin)


def norm_forward(hidden, gain, bias):
    centered = hidden - jnp.mean(hidden, axis=-1, keepdims=True)
    inv_std = lax.rsqrt(jnp.mean(centered * centered, axis=-1, keepdims=True) + EPSILON)
    normed = centered * inv_std
    return normed * gain + bias, normed, inv_std


def norm_back(grad_y, normed, inv_std, gain):
    grad_gain = jnp.sum(grad_y * normed, axis=0)
    grad_bias = jnp.sum(grad_y, axis=0)
    scaled = grad_y * gain
    grad_h = inv_std * (
        scaled
        - jnp.mean(scaled, axis=-1, keepdims=True)
        - normed * jnp.mean(scaled * normed, axis=-1, keepdims=True)
    )
    return grad_h, grad_gain, grad_bias


def on_device(
    mp,
    inputs,
    segments,
    w_qkv,
    w_out,
    first_gain,
    first_bias,
    w_gate,
    w_up,
    w_down,
    second_gain,
    second_bias,
    d_out,
):
    group = ("chip", "mp")
    crossing = [(a * mp + b, b * mp + a) for a in range(2) for b in range(mp)]

    def cross(tensor):
        return lax.ppermute(tensor, ("core", "mp"), crossing)

    def mate(tensor):
        return lax.ppermute(tensor, "core", [(0, 1), (1, 0)])

    core = lax.axis_index("core")
    shard, half_cols = w_qkv.shape[1], w_qkv.shape[2]
    pairs = half_cols // LANES
    width = inputs.shape[1]
    half_ff = w_gate.shape[1]
    half_len = inputs.shape[0]
    turn = core * half_len

    vectors = jnp.stack([first_gain, first_bias, second_gain, second_bias], axis=1)
    pad = jnp.zeros((shard, LANES - 4), BF16)
    attn_shard = jnp.concatenate(
        [
            w_qkv.reshape(3, shard, pairs, LANES).transpose(1, 2, 0, 3).reshape(shard, 3 * half_cols),
            w_out.T,
            vectors,
            pad,
        ],
        axis=1,
    )
    ff_shard = jnp.concatenate([w_gate, w_up, w_down.T], axis=1)
    attn_w = lax.all_gather(cross(attn_shard), group, axis=0, tiled=True)
    rows_own = cross(inputs)
    labels = cross(segments)
    ff_own = lax.all_gather(cross(ff_shard), group, axis=0, tiled=True)
    ff_mate = mate(ff_own)
    d_own = cross(d_out)

    rows_all = jnp.concatenate([rows_own, mate(rows_own)], axis=0)
    labels = jnp.where(core == 0, labels, jnp.roll(labels, half_len))
    qkv_w = attn_w[:, : 3 * half_cols]
    out_own = attn_w[:, 3 * half_cols : 4 * half_cols]
    out_mate = mate(out_own)
    gains = attn_w[:, 4 * half_cols : 4 * half_cols + 4].astype(F32).T
    gain_one, bias_one, gain_two, bias_two = gains[0], gains[1], gains[2], gains[3]
    cos, sin = (jnp.asarray(t) for t in rope_tables())

    qkv = project(core.reshape(1), rows_all, qkv_w, cos, sin)
    o, lse = attend(qkv, labels, turn)
    o_in = mate(o[half_len:])
    attn = dot(o[:half_len], out_own, NT) + dot(o_in, out_mate, NT)
    middle, first_hat, first_inv = norm_forward(rows_own.astype(F32) + attn, gain_one, bias_one)
    middle_low = middle.astype(BF16)

    saved = []
    mlp = None
    for block in (ff_own, ff_mate):
        gate_w, up_w, down_t = (block[:, k * half_ff : (k + 1) * half_ff] for k in range(3))
        gate = dot(middle_low, gate_w)
        up = dot(middle_low, up_w)
        sig = jax.nn.sigmoid(gate)
        silu = gate * sig
        hidden = (silu * up).astype(BF16)
        part = dot(hidden, down_t, NT)
        mlp = part if mlp is None else mlp + part
        saved.append((gate_w, up_w, down_t, gate, up, sig, silu, hidden))
    result, second_hat, second_inv = norm_forward(middle + mlp, gain_two, bias_two)
    outputs = cross(result.astype(BF16))
    grad_two, second_gain_part, second_bias_part = norm_back(
        d_own.astype(F32), second_hat, second_inv, gain_two
    )
    grad_two_low = grad_two.astype(BF16)
    grad_middle = grad_two
    grads = []
    for gate_w, up_w, down_t, gate, up, sig, silu, hidden in saved:
        grad_down_t = dot(grad_two_low, hidden, TN)
        grad_hidden = dot(grad_two_low, down_t)
        grad_gate = (grad_hidden * up * sig * (1.0 + gate * (1.0 - sig))).astype(BF16)
        grad_up = (grad_hidden * silu).astype(BF16)
        grads.append((dot(middle_low, grad_gate, TN), dot(middle_low, grad_up, TN), grad_down_t))
        grad_middle = grad_middle + dot(grad_gate, gate_w, NT) + dot(grad_up, up_w, NT)
    grad_one, first_gain_part, first_bias_part = norm_back(grad_middle, first_hat, first_inv, gain_one)
    sums = jnp.stack([first_gain_part, first_bias_part, second_gain_part, second_bias_part], axis=1)
    sums = jnp.concatenate([sums, jnp.zeros((width, LANES - 4), F32)], axis=1)
    ff_grad = jnp.concatenate([*grads[0], sums], axis=1)
    ff_sent = mate(jnp.concatenate([*grads[1], sums], axis=1).astype(BF16))
    ff_grad = (ff_grad + ff_sent.astype(F32)).astype(BF16)
    ff_grad = cross(lax.psum_scatter(ff_grad, group, scatter_dimension=0, tiled=True)).astype(F32)

    grad_one_low = grad_one.astype(BF16)
    grad_one_all = jnp.concatenate([grad_one_low, mate(grad_one_low)], axis=0)
    grad_one_home = cross(grad_one)
    do = dot(grad_one_all, out_own).astype(BF16)
    grad_out_t = dot(grad_one_all, o, TN).astype(BF16)
    cos_turned, sin_turned = (
        jnp.where(core == 0, t, jnp.roll(t, half_len, axis=0)) for t in (cos, sin)
    )
    grad_rows = None
    weight_grads = []
    for pair in range(pairs):
        back = attend_back(pair, qkv, o, do, lse, labels, turn, cos_turned, sin_turned)
        weight_grads.append(dot(rows_all, back, TN).astype(BF16))
        part = dot(back, qkv_w[:, pair * 3 * LANES : (pair + 1) * 3 * LANES], NT)
        grad_rows = part if grad_rows is None else grad_rows + part
    grad_rows = grad_rows[:half_len] + mate(grad_rows[half_len:].astype(BF16)).astype(F32)
    grad_inputs = grad_one_home + cross(grad_rows.astype(BF16)).astype(F32)
    attn_grad = jnp.concatenate([*weight_grads, grad_out_t], axis=1)
    attn_grad = cross(lax.psum_scatter(attn_grad, group, scatter_dimension=0, tiled=True)).astype(F32)

    grad_qkv = (
        attn_grad[:, : 3 * half_cols]
        .reshape(shard, pairs, 3, LANES)
        .transpose(2, 0, 1, 3)
        .reshape(3, shard, half_cols)
    )
    grad_out = attn_grad[:, 3 * half_cols :].T
    grad_gate, grad_up, grad_down_t = (ff_grad[:, k * half_ff : (k + 1) * half_ff] for k in range(3))
    grad_vectors = ff_grad[:, 3 * half_ff : 3 * half_ff + 4]
    return (
        outputs,
        grad_inputs,
        grad_qkv,
        grad_out,
        grad_vectors[:, 0],
        grad_vectors[:, 1],
        grad_gate,
        grad_up,
        grad_down_t.T,
        grad_vectors[:, 2],
        grad_vectors[:, 3],
    )


def solution(mesh):
    dp, mp = mesh.shape["dp"], mesh.shape["mp"]
    split = Mesh(mesh.devices.reshape(dp // 2, 2, mp), ("chip", "core", "mp"))
    rows = P(("chip", "core", "mp"), None)
    vector = P(("chip", "core"))
    columns = P(("chip", "core"), "mp")
    turned = P("mp", ("chip", "core"))
    stacked = P(None, ("chip", "core"), "mp")
    return jax.shard_map(
        functools.partial(on_device, mp),
        mesh=split,
        in_specs=(
            rows,
            vector,
            stacked,
            turned,
            vector,
            vector,
            columns,
            columns,
            turned,
            vector,
            vector,
            rows,
        ),
        out_specs=(
            rows,
            rows,
            stacked,
            turned,
            vector,
            vector,
            columns,
            columns,
            turned,
            vector,
            vector,
        ),
        check_vma=False,
    )
```

time: 1800 us -> 823 us (0.46)
  waiting for transfers between devices: 838 us -> 359 us
  matrix products: 438 us -> 129 us
  local copies, waits for them, and re-layouts: 218 us -> 70.7 us
  Pallas kernels: 0 us -> 132 us
  blocking collectives: 126 us -> 0 us
  starting transfers between devices: 0.69 us -> 68.2 us
  loops' own time: 60 us -> 0 us
  other arithmetic: 93.3 us -> 43.1 us
    reduce_scatter x8 -> x1, waiting for transfers between devices: 535 us -> 155 us  [on_device(): lax.psum_scatter(ff_grad, group, scatter_dimension=0, tiled=True)]
    dot_general x183 -> x28, matrix products: 438 us -> 129 us  [dot(): return lax.dot_general(left, right, dims, preferred_element_type=F32)]
    all_gather x8 -> x2, waiting for transfers between devices: 300 us -> 121 us  [the longest x1 61.6 us: on_device(): ff_own = lax.all_gather(cross(ff_shard), group, axis=0, tiled=True)]
    pallas_call x0 -> x5, Pallas kernels: none -> 132 us  [the longest x3 80.7 us: attend_back(): pl.pallas_call(functools.partial(attend_back_kernel, turn_steps=0), grid_...]
    unnamed x2 -> x0, blocking collectives: 94.3 us -> none
    unnamed x18 -> x5, waiting for transfers between devices: 3.7 us -> 82.9 us
    ppermute x0 -> x17, starting transfers between devices: none -> 68.1 us  [the longest x10 42.3 us: cross(): return lax.ppermute(tensor, ('core', 'mp'), crossing)]
    while x410 -> x0, local copies, waits for them, and re-layouts: 64.2 us -> none
  transfers between devices with their start and end apart: 17 -> 21, of which waited for: 17 -> 5; matrix products, arithmetic and copies ran while one was open for 5% -> 21% of each run, Pallas kernels for 0% -> 16%
where the time goes in v1:
time: 823 us; the launch traced here: 817 us
  waiting for transfers between devices  359 us (44%)
  Pallas kernels  132 us (16%)
  matrix products  129 us (16%)
  local copies, waits for them, and re-layouts  70.7 us (9%)
  starting transfers between devices  68.2 us (8%)
  other arithmetic  43.1 us (5%)
  between operations  14.8 us (2%)
    reduce_scatter x1, waiting for transfers between devices, on_device(): lax.psum_scatter(ff_grad, group, scatter_dimension=0, tiled=True)  155 us
    dot_general x28, matrix products, dot(): return lax.dot_general(left, right, dims, preferred_element_type=F32)  129 us
    unnamed x5, waiting for transfers between devices  82.9 us
    pallas_call x3, Pallas kernels, attend_back(): pl.pallas_call(functools.partial(attend_back_kernel, turn_steps=0), grid_...  80.7 us
    all_gather x1, waiting for transfers between devices, on_device(): ff_own = lax.all_gather(cross(ff_shard), group, axis=0, tiled=True)  61.6 us
    all_gather x1, waiting for transfers between devices, on_device(): attn_w = lax.all_gather(cross(attn_shard), group, axis=0, tiled=True)  59.6 us
    ppermute x10, starting transfers between devices, cross(): return lax.ppermute(tensor, ('core', 'mp'), crossing)  42.3 us
    pallas_call x1, Pallas kernels, attend(): pl.pallas_call(attend_kernel, grid_spec=pltpu.PrefetchScalarGridSpec(num_...  39.7 us
  transfers between devices with their start and end apart: 21, of which 5 were waited for; matrix products, arithmetic and copies ran while one was open for 21% of the time, Pallas kernels for 16%

profile of v1, /device:TPU:0, one launch (start us, length us, event | category | flops | bytes accessed | tf_op | source)
XLA Modules:
  0.0 816.6 jit_solution(8581821389599801836)
XLA Ops:
  19.9 13.3 %collective-permute-start.9 = (bf16[1024,768]{1,0:T(8,128)(2,1)}, bf16[1024,768]{1,0:T(8,128)(2,1)}, u32[]{:S(2)}, u32[]{:S(2)}) collective-permute-start(bf16[1024,768]{1,0:T(8,128)(2,1)} %param.25), channel_id=1, source_target_pairs={{0,0},{1,2},{2,1},{3,3},{4,4},{5,6},{6,5},{7,7},{8,8},{9,10},{10,9... | collective-permute-start | bytes 4718600 | tf_op jit(solution)/shard_map/ppermute | solution.py:346
  36.0 24.3 %collective-permute-start.2 = (bf16[1024,768]{1,0:T(8,128)(2,1)S(1)}, bf16[1024,768]{1,0:T(8,128)(2,1)S(1)}, u32[]{:S(2)}, u32[]{:S(2)}) collective-permute-start(bf16[1024,768]{1,0:T(8,128)(2,1)S(1)} %collective-permute-done), channel_id=1, source_target_pairs={{0,2},{2,0},{1,3},{3,1},{4,6},{6,4},{5,7},{7,5},{8,10},{10,8},{9,1... | collective-permute-start | bytes 4718600 | tf_op jit(solution)/shard_map/ppermute | solution.py:349
  61.4 61.6 %all-gather.5.cloned.1.call-done = bf16[768,4608]{1,0:T(8,128)(2,1)} async-done(((bf16[48,4608]{1,0:T(8,128)(2,1)}), bf16[768,4608]{1,0:T(8,128)(2,1)}) %all-gather.5.cloned.1.call-update) | async-done | bytes 7077904 | tf_op jit(solution)/shard_map/all_gather | solution.py:374
  128.3 59.6 %all-gather.3.cloned.1.call-done = bf16[768,1664]{1,0:T(8,128)(2,1)} async-done(((bf16[48,1664]{1,0:T(8,128)(2,1)}), bf16[768,1664]{1,0:T(8,128)(2,1)}) %all-gather.3.cloned.1.call-update) | async-done | bytes 2555920 | tf_op jit(solution)/shard_map/all_gather | solution.py:371
  190.8 11.3 %project.1.q_ref.k_ref.v_ref = bf16[2048,1152]{1,0:T(8,128)(2,1)} custom-call(s32[1]{0:T(128)} %bitcast.core_ref, bf16[2048,768]{1,0:T(8,128)(2,1)} %constant_dynamic-update-slice_fusion.x_ref, bf16[768,1152]{1,0:T(8,128)(2,1)} %slice.166.w_ref, f32[2048,128]{1,0:T(8,128)} %constant.124.clone.cos_ref, f32[2048,128]{1,0:T(8,128)} %constant.125.clone.sin_ref), custom_call_target="tpu_custom_call" | custom-call | flops 3623878656 | bytes 9633792 | tf_op jit(solution)/shard_map/project/pallas_call | solution.py:78
  202.1 39.7 %attend.1 = (bf16[2048,384]{1,0:T(8,128)(2,1)}, f32[3,2,2048]{2,1,0:T(2,128)}) custom-call(s32[2]{0:T(128)} %broadcast_add_fusion.1.low_ref, s32[2]{0:T(128)} %get-tuple-element.107.high_ref, bf16[2048,1152]{1,0:T(8,128)(2,1)} %project.1.q_ref.k_ref.v_ref, bf16[2048,1152]{1,0:T(8,128)(2,1)} %project.1.q_ref.k_ref.v_ref, ...), custom_call_target="tpu_custom_call" | custom-call | flops 12884901888 | bytes 6291456 | tf_op jit(solution)/shard_map/attend/pallas_call | solution.py:169
  252.2 5.2 multiply_convert_fusion.5
  257.4 5.4 fusion.21
  262.8 8.7 %multiply_convert_fusion.4 = (bf16[1024,1536]{1,0:T(8,128)(2,1)S(1)}, f32[1024,1536]{1,0:T(8,128)}) fusion(f32[1024,1536]{1,0:T(8,128)S(1)} %fusion.21, bf16[1024,768]{1,0:T(8,128)(2,1)S(1)} %fusion.10, bf16[768,4608]{1,0:T(8,128)(2,1)} %collective-permute-done.7), kind=kOutput, calls=%fused_computation.6 | convolution fusion | flops 2425356288 | bytes 19660800 | tf_op jit(solution)/shard_map/dot_general | solution.py:31
  271.5 5.4 fusion.13
  287.4 9.6 %multiply_convert_fusion = (bf16[1024,1536]{1,0:T(8,128)(2,1)}, bf16[1024,1536]{1,0:T(8,128)(2,1)S(1)}) fusion(f32[1024,1536]{1,0:T(8,128)} %copy-done.40, f32[1024,1536]{1,0:T(8,128)} %get-tuple-element.122, bf16[1024,768]{1,0:T(8,128)(2,1)S(1)} %get-tuple-element.113, bf16[768,4608]{1,0:T(8,128)(2,1)} %collective-permute-done.7), kind=kOutput, calls=%fused_computation.2 | convolution fusion | flops 2436366336 | bytes 22806528 | tf_op jit(solution)/shard_map/dot_general | solution.py:31
  296.9 8.8 %multiply_convert_fusion.3 = (bf16[1024,1536]{1,0:T(8,128)(2,1)S(1)}, bf16[1024,1536]{1,0:T(8,128)(2,1)S(1)}) fusion(f32[1024,1536]{1,0:T(8,128)} %copy-done.39, f32[1024,1536]{1,0:T(8,128)} %get-tuple-element.124, bf16[1024,768]{1,0:T(8,128)(2,1)S(1)} %get-tuple-element.113, bf16[768,4608]{1,0:T(8,128)(2,1)S(1)} %bitcast.70), kind=kOutput, calls=%fused_computation.5 | convolution fusion | flops 2436366336 | bytes 22806528 | tf_op jit(solution)/shard_map/dot_general | solution.py:31
  305.8 4.2 fusion.31
  310.1 4.3 fusion.27
  314.4 6.1 fusion.19
  320.5 8.9 %multiply_reduce_fusion = (f32[768]{0:T(1024)S(1)}, f32[1024]{0:T(1024)}, f32[1024]{0:T(1024)}, f32[768]{0:T(1024)S(1)}, f32[1024,768]{1,0:T(8,128)}) fusion(f32[1024,768]{1,0:T(8,128)S(1)} %get-tuple-element.120, f32[1024]{0:T(1024)S(1)} %add_rsqrt_fusion.1, f32[1024]{0:T(1024)S(1)} %broadcast_multiply_fusion.5, f32[768]{0:T(1024)S(1)} %get-tuple-element.96, ...), kind=kOutput, calls=%fused_computation.29 | convolution fusion | flops 2432430592 | bytes 25997312 | tf_op jit(solution)/shard_map/dot_general | solution.py:31
  355.1 12.4 %concatenate.45 = bf16[768,4736]{1,0:T(8,128)(2,1)} concatenate(bf16[768,1536]{1,0:T(8,128)(2,1)} %convolution_convert_fusion.2, bf16[768,1536]{1,0:T(8,128)(2,1)} %convolution_convert_fusion.1, bf16[768,1536]{1,0:T(8,128)(2,1)} %convolution_convert_fusion, bf16[768,1]{1,0:T(8,128)(2,1)S(1)} %copy.146, bf16[768,1]{1,0:T(8,128)(2,1)S(1)} %copy.147, bf16[768,1]{1,0:T(8,128)(2,1)} %copy.148, ...), dimensions={1} | concatenate | bytes 14548992 | tf_op jit(solution)/shard_map/concatenate | solution.py:425
  371.3 5.0 convolution_convert_fusion.3.do_ref
  376.3 26.8 %attend_back.5 = bf16[2048,384]{1,0:T(8,128)(2,1)} custom-call(s32[4]{0:T(128)} %broadcast_add_fusion.low_ref, s32[4]{0:T(128)} %get-tuple-element.103.high_ref, bf16[2048,1152]{1,0:T(8,128)(2,1)} %project.1.q_ref.k_ref.v_ref, bf16[2048,1152]{1,0:T(8,128)(2,1)} %project.1.q_ref.k_ref.v_ref, bf16[2048,1152]{1,0:T(8,128)(2,1)} %project.1.q_ref.k_ref.v_ref, ...), custom_call_target="tpu_custom_call" | custom-call | flops 10737418240 | bytes 4194304 | tf_op jit(solution)/shard_map/attend_back/pallas_call | solution.py:273
  406.9 27.1 %attend_back.4 = bf16[2048,384]{1,0:T(8,128)(2,1)} custom-call(s32[4]{0:T(128)} %broadcast_add_fusion.low_ref, s32[4]{0:T(128)} %get-tuple-element.103.high_ref, bf16[2048,1152]{1,0:T(8,128)(2,1)} %project.1.q_ref.k_ref.v_ref, bf16[2048,1152]{1,0:T(8,128)(2,1)} %project.1.q_ref.k_ref.v_ref, bf16[2048,1152]{1,0:T(8,128)(2,1)} %project.1.q_ref.k_ref.v_ref, ...), custom_call_target="tpu_custom_call" | custom-call | flops 10737418240 | bytes 4194304 | tf_op jit(solution)/shard_map/attend_back/pallas_call | solution.py:273
  437.7 26.8 %attend_back.3 = bf16[2048,384]{1,0:T(8,128)(2,1)} custom-call(s32[4]{0:T(128)} %broadcast_add_fusion.low_ref, s32[4]{0:T(128)} %get-tuple-element.103.high_ref, bf16[2048,1152]{1,0:T(8,128)(2,1)} %project.1.q_ref.k_ref.v_ref, bf16[2048,1152]{1,0:T(8,128)(2,1)} %project.1.q_ref.k_ref.v_ref, bf16[2048,1152]{1,0:T(8,128)(2,1)} %project.1.q_ref.k_ref.v_ref, ...), custom_call_target="tpu_custom_call" | custom-call | flops 10737418240 | bytes 4194304 | tf_op jit(solution)/shard_map/attend_back/pallas_call | solution.py:273
  469.9 4.3 copy.155
  478.6 6.5 fusion.67
  485.1 4.4 fusion.65
  489.5 4.4 fusion.66
  494.0 15.8 %concatenate.44 = f32[768,4736]{1,0:T(8,128)} concatenate(f32[768,1536]{1,0:T(8,128)} %fusion.65, f32[768,1536]{1,0:T(8,128)} %fusion.66, f32[768,1536]{1,0:T(8,128)} %fusion.67, f32[768,1]{1,0:T(8,128)S(1)} %copy.142, f32[768,1]{1,0:T(8,128)S(1)} %copy-done.16, f32[768,1]{1,0:T(8,128)S(1)} %copy-done.17, f32[768,1]{1,0:T(8,128)S(1)} %copy-done.18, f32[768,124]{1,0:T(8,128)S(1)} %broadcast_in_dim.21), dimensions={1} | concatenate | bytes 29097984 | tf_op jit(solution)/shard_map/concatenate | solution.py:424
  509.8 10.8 %add_convert_fusion = bf16[768,4736]{1,0:T(8,128)(2,1)} fusion(f32[768,4736]{1,0:T(8,128)} %concatenate.44, bf16[768,4736]{1,0:T(8,128)(2,1)} %collective-permute-done.15), kind=kLoop, calls=%fused_computation | loop fusion | flops 10911744 | bytes 29097984 | tf_op jit(solution)/shard_map/convert_element_type | solution.py:426
  537.1 13.4 %collective-permute-start.13 = (bf16[1024,768]{1,0:T(8,128)(2,1)}, bf16[1024,768]{1,0:T(8,128)(2,1)}, u32[]{:S(2)}, u32[]{:S(2)}) collective-permute-start(bf16[1024,768]{1,0:T(8,128)(2,1)} %fusion.9), channel_id=1, source_target_pairs={{0,0},{1,2},{2,1},{3,3},{4,4},{5,6},{6,5},{7,7},{8,8},{9,10},{10,9... | collective-permute-start | bytes 4718600 | tf_op jit(solution)/shard_map/ppermute | solution.py:346
  550.4 82.8 %reduce-scatter.7.cloned.1.call-done = bf16[48,1536]{1,0:T(8,128)(2,1)} async-done(((bf16[768,1536]{1,0:T(8,128)(2,1)}), bf16[48,1536]{1,0:T(8,128)(2,1)}) %reduce-scatter.7.cloned.1.call-update) | async-done | bytes 147472
  636.7 154.6 %reduce-scatter.5.cloned.1.call-done = bf16[48,4736]{1,0:T(8,128)(2,1)} async-done(((bf16[768,4736]{1,0:T(8,128)(2,1)}), bf16[48,4736]{1,0:T(8,128)(2,1)}) %reduce-scatter.5.cloned.1.call-update) | async-done | bytes 454672 | tf_op jit(solution)/shard_map/reduce_scatter | solution.py:427
  791.3 5.0 collective-permute-start.16
  796.3 4.3 convert_add_fusion
  (219 shorter events, 120.7 us)
Async XLA Ops:
  7.2 26.0 %copy-start.23 = (f32[2048,128]{1,0:T(8,128)S(1)}, f32[2048,128]{1,0:T(8,128)}, u32[]{:S(2)}) copy-start(f32[2048,128]{1,0:T(8,128)} %constant.124.clone.cos_ref) | copy-start | bytes 3145732
  7.2 115.8 %all-gather.5.cloned.1.call-start = ((), (), s32[]{:S(2)}) async-start(), calls=%async_computation.3 | async-start | bytes 7520256 | tf_op jit(solution)/shard_map/all_gather | solution.py:374
  8.4 0.7 collective-permute-start.6
  9.9 178.1 %all-gather.3.cloned.1.call-start = ((), (), s32[]{:S(2)}) async-start(), calls=%async_computation.2 | async-start | bytes 2715648 | tf_op jit(solution)/shard_map/all_gather | solution.py:371
  15.0 0.7 collective-permute-start.3
  16.4 616.8 %reduce-scatter.7.cloned.1.call-start = ((), (), s32[]{:S(2)}) async-start(), calls=%async_computation.5 | async-start | bytes 2506752
  16.4 19.5 %collective-permute-start = (bf16[1024,768]{1,0:T(8,128)(2,1)}, bf16[1024,768]{1,0:T(8,128)(2,1)S(1)}, u32[]{:S(2)}, u32[]{:S(2)}) collective-permute-start(bf16[1024,768]{1,0:T(8,128)(2,1)} %param.14), channel_id=1, source_target_pairs={{0,0},{1,2},{2,1},{3,3},{4,4},{5,6},{6,5},{7,7},{8,8},{9,10},{10,9... | collective-permute-start | bytes 4718600 | tf_op jit(solution)/shard_map/ppermute | solution.py:346
  18.5 41.7 %collective-permute-start.1 = (s32[2048]{0:T(1024)}, s32[2048]{0:T(1024)S(1)}, u32[]{:S(2)}, u32[]{:S(2)}) collective-permute-start(s32[2048]{0:T(1024)} %param.15), channel_id=1, source_target_pairs={{0,0},{1,2},{2,1},{3,3},{4,4},{5,6},{6,5},{7,7},{8,8},{9,10},{10,9... | collective-permute-start | bytes 24584 | tf_op jit(solution)/shard_map/ppermute | solution.py:346
  19.9 260.7 %collective-permute-start.9 = (bf16[1024,768]{1,0:T(8,128)(2,1)}, bf16[1024,768]{1,0:T(8,128)(2,1)}, u32[]{:S(2)}, u32[]{:S(2)}) collective-permute-start(bf16[1024,768]{1,0:T(8,128)(2,1)} %param.25), channel_id=1, source_target_pairs={{0,0},{1,2},{2,1},{3,3},{4,4},{5,6},{6,5},{7,7},{8,8},{9,10},{10,9... | collective-permute-start | bytes 4718600 | tf_op jit(solution)/shard_map/ppermute | solution.py:346
  36.0 92.4 %copy-start.7 = (bf16[1024,768]{1,0:T(8,128)(2,1)}, bf16[1024,768]{1,0:T(8,128)(2,1)S(1)}, u32[]{:S(2)}) copy-start(bf16[1024,768]{1,0:T(8,128)(2,1)S(1)} %collective-permute-done) | copy-start | bytes 4718596
  36.0 91.1 %collective-permute-start.2 = (bf16[1024,768]{1,0:T(8,128)(2,1)S(1)}, bf16[1024,768]{1,0:T(8,128)(2,1)S(1)}, u32[]{:S(2)}, u32[]{:S(2)}) collective-permute-start(bf16[1024,768]{1,0:T(8,128)(2,1)S(1)} %collective-permute-done), channel_id=1, source_target_pairs={{0,2},{2,0},{1,3},{3,1},{4,6},{6,4},{5,7},{7,5},{8,10},{10,8},{9,1... | collective-permute-start | bytes 4718600 | tf_op jit(solution)/shard_map/ppermute | solution.py:349
  123.0 134.4 %collective-permute-start.7 = (bf16[768,4608]{1,0:T(8,128)(2,1)}, bf16[768,4608]{1,0:T(8,128)(2,1)}, u32[]{:S(2)}, u32[]{:S(2)}) collective-permute-start(bf16[768,4608]{1,0:T(8,128)(2,1)} %all-gather.5.cloned.1.call-done), channel_id=1, source_target_pairs={{0,2},{2,0},{1,3},{3,1},{4,6},{6,4},{5,7},{7,5},{8,10},{10,8},{9,1... | collective-permute-start | bytes 21233672 | tf_op jit(solution)/shard_map/ppermute | solution.py:349
  202.1 41.6 %copy-start.2 = (bf16[768,1664]{1,0:T(8,128)(2,1)S(1)}, bf16[768,1664]{1,0:T(8,128)(2,1)}, u32[]{:S(2)}) copy-start(bf16[768,1664]{1,0:T(8,128)(2,1)} %all-gather.3.cloned.1.call-done) | copy-start | bytes 7667716
  243.1 3.2 collective-permute-start.4
  243.7 2.5 collective-permute-start.5
  249.6 13.2 %copy-start = (bf16[1024,768]{1,0:T(8,128)(2,1)}, bf16[1024,768]{1,0:T(8,128)(2,1)S(1)}, u32[]{:S(2)}) copy-start(bf16[1024,768]{1,0:T(8,128)(2,1)S(1)} %fusion.10) | copy-start | bytes 4718596
  257.4 19.5 %copy-start.9 = (bf16[1024,1536]{1,0:T(8,128)(2,1)}, bf16[1024,1536]{1,0:T(8,128)(2,1)S(1)}, u32[]{:S(2)}) copy-start(bf16[1024,1536]{1,0:T(8,128)(2,1)S(1)} %get-tuple-element.123) | copy-start | bytes 9437188
  262.8 8.7 %copy-start.40 = (f32[1024,1536]{1,0:T(8,128)}, f32[1024,1536]{1,0:T(8,128)S(1)}, u32[]{:S(2)}) copy-start(f32[1024,1536]{1,0:T(8,128)S(1)} %fusion.21) | copy-start | bytes 18874372
  287.4 9.6 %copy-start.4 = (bf16[1024,768]{1,0:T(8,128)(2,1)}, bf16[1024,768]{1,0:T(8,128)(2,1)S(1)}, u32[]{:S(2)}) copy-start(bf16[1024,768]{1,0:T(8,128)(2,1)S(1)} %get-tuple-element.113) | copy-start | bytes 4718596
  296.9 17.4 %copy-start.33 = (bf16[1024,1536]{1,0:T(8,128)(2,1)}, bf16[1024,1536]{1,0:T(8,128)(2,1)S(1)}, u32[]{:S(2)}) copy-start(bf16[1024,1536]{1,0:T(8,128)(2,1)S(1)} %get-tuple-element.110) | copy-start | bytes 9437188
  342.1 25.8 %collective-permute-start.11 = (bf16[1024,768]{1,0:T(8,128)(2,1)}, bf16[1024,768]{1,0:T(8,128)(2,1)}, u32[]{:S(2)}, u32[]{:S(2)}) collective-permute-start(bf16[1024,768]{1,0:T(8,128)(2,1)} %get-tuple-element.101), channel_id=1, source_target_pairs={{0,2},{2,0},{1,3},{3,1},{4,6},{6,4},{5,7},{7,5},{8,10},{10,8},{9,1... | collective-permute-start | bytes 4718600 | tf_op jit(solution)/shard_map/ppermute | solution.py:349
  355.1 12.9 %copy-start.21 = (bf16[2048,384]{1,0:T(8,128)(2,1)S(1)}, bf16[2048,384]{1,0:T(8,128)(2,1)}, u32[]{:S(2)}) copy-start(bf16[2048,384]{1,0:T(8,128)(2,1)} %get-tuple-element.13.o_ref) | copy-start | bytes 4718596
  367.5 142.3 %collective-permute-start.15 = (bf16[768,4736]{1,0:T(8,128)(2,1)}, bf16[768,4736]{1,0:T(8,128)(2,1)}, u32[]{:S(2)}, u32[]{:S(2)}) collective-permute-start(bf16[768,4736]{1,0:T(8,128)(2,1)} %concatenate.45), channel_id=1, source_target_pairs={{0,2},{2,0},{1,3},{3,1},{4,6},{6,4},{5,7},{7,5},{8,10},{10,8},{9,1... | collective-permute-start | bytes 21823496 | tf_op jit(solution)/shard_map/ppermute | solution.py:349
  474.2 317.0 %reduce-scatter.5.cloned.1.call-start = ((), (), s32[]{:S(2)}) async-start(), calls=%async_computation.4 | async-start | bytes 7729152 | tf_op jit(solution)/shard_map/reduce_scatter | solution.py:427
  478.6 6.5 copy-start.14
  527.5 6.1 copy-start.22
  529.6 5.9 collective-permute-start.12
  531.4 264.9 %collective-permute-start.10 = (f32[1024,768]{1,0:T(8,128)S(1)}, f32[1024,768]{1,0:T(8,128)}, u32[]{:S(2)}, u32[]{:S(2)}) collective-permute-start(f32[1024,768]{1,0:T(8,128)S(1)} %copy-done.10), channel_id=1, source_target_pairs={{0,0},{1,2},{2,1},{3,3},{4,4},{5,6},{6,5},{7,7},{8,8},{9,10},{10,9... | collective-permute-start | bytes 9437192 | tf_op jit(solution)/shard_map/ppermute | solution.py:346
  533.7 16.8 %collective-permute-start.8 = (bf16[1024,768]{1,0:T(8,128)(2,1)S(1)}, bf16[1024,768]{1,0:T(8,128)(2,1)}, u32[]{:S(2)}, u32[]{:S(2)}) collective-permute-start(bf16[1024,768]{1,0:T(8,128)(2,1)S(1)} %copy-done.22), channel_id=1, source_target_pairs={{0,0},{1,2},{2,1},{3,3},{4,4},{5,6},{6,5},{7,7},{8,8},{9,10},{10,9... | collective-permute-start | bytes 4718600 | tf_op jit(solution)/shard_map/ppermute | solution.py:346
  537.1 259.3 %collective-permute-start.13 = (bf16[1024,768]{1,0:T(8,128)(2,1)}, bf16[1024,768]{1,0:T(8,128)(2,1)}, u32[]{:S(2)}, u32[]{:S(2)}) collective-permute-start(bf16[1024,768]{1,0:T(8,128)(2,1)} %fusion.9), channel_id=1, source_target_pairs={{0,0},{1,2},{2,1},{3,3},{4,4},{5,6},{6,5},{7,7},{8,8},{9,10},{10,9... | collective-permute-start | bytes 4718600 | tf_op jit(solution)/shard_map/ppermute | solution.py:346
  635.1 165.6 %collective-permute-start.14 = (bf16[48,1536]{0,1:T(8,128)(2,1)}, bf16[48,1536]{0,1:T(8,128)(2,1)S(1)}, u32[]{:S(2)}, u32[]{:S(2)}) collective-permute-start(bf16[48,1536]{0,1:T(8,128)(2,1)} %copy.156), channel_id=1, source_target_pairs={{0,0},{1,2},{2,1},{3,3},{4,4},{5,6},{6,5},{7,7},{8,8},{9,10},{10,9... | collective-permute-start | bytes 442376 | tf_op jit(solution)/shard_map/ppermute | solution.py:346
  791.3 11.3 %collective-permute-start.16 = (bf16[48,4736]{1,0:T(8,128)(2,1)}, bf16[48,4736]{1,0:T(8,128)(2,1)}, u32[]{:S(2)}, u32[]{:S(2)}) collective-permute-start(bf16[48,4736]{1,0:T(8,128)(2,1)} %reduce-scatter.5.cloned.1.call-done), channel_id=1, source_target_pairs={{0,0},{1,2},{2,1},{3,3},{4,4},{5,6},{6,5},{7,7},{8,8},{9,10},{10,9... | collective-permute-start | bytes 1363976 | tf_op jit(solution)/shard_map/ppermute | solution.py:346
  (32 other events, 116.1 us)
Sparse Core Ops, SparseCore 0:
  11.4 111.5 all-gather.4
  126.4 61.5 all-gather.2
  474.3 158.8 reduce-scatter.6
  639.3 151.9 reduce-scatter.4
